TPU v7x, 32 devices: a whole 2x2x4 slice. The times are simulated.
32 devices in a mesh: dp: 1, center: 32 (over z, y, x, core).
Axes of the slice: x: 2, y: 2, z: 4, core: 2. Of those that a mesh axis runs over, the one named last changes fastest.
Arguments:
- embeddings: bfloat16 [1024, 2048], P('dp', 'center'), may hold values from -6 to 6
- first_weight: bfloat16 [2048, 2048], P(None, 'center'), may hold values from -0.125 to 0.125
- first_bias: float32 [2048], P('center'), may hold values from -3 to 3
- second_weight: bfloat16 [2048, 512], P('center'), may hold values from -0.1875 to 0.1875
- centers: bfloat16 [65536, 512], P('center'), may hold values from -4 to 4
- coefficients: bfloat16 [65536, 100], P('center'), may hold values from -12 to 12
- cotangent: bfloat16 [1024, 100], P('dp'), may hold values from -18 to 18
Outputs:
- predictions: float32 [1024, 100], P(('dp', 'center'))
- grad_first: float32 [2048, 2048], P('dp', 'center')
- grad_bias: float32 [2048], P('center')
- grad_second: float32 [2048, 512], P('center', 'dp')
- grad_centers: float32 [65536, 512], P('center', 'dp')
- grad_coefs: float32 [65536, 100], P('center')
All inputs are finite; a program needn't handle non-finite values.
Results may differ from a plain program's by a relative error of at most 0.028.
Values may be sent and summed in bfloat16 or wider, within the bound.
No kernel may reach another device: no remote copies, remote signals or barrier semaphores. Data moves between devices by JAX's collectives and lax.ppermute only.
A program may use at most 64 MiB of HBM per device.

v0:
```python
import jax
import jax.numpy as jnp
from jax import lax
from jax.sharding import PartitionSpec as P


def body(embeddings, first_weight, first_bias, second_weight, centers, coefficients, cotangent):
    feat_width = centers.shape[1]
    factor = 16.0 / feat_width
    gathered = lax.all_gather(embeddings, "center", axis=1, tiled=True)
    preact = jnp.dot(gathered, first_weight, preferred_element_type=jnp.float32) + first_bias
    hidden = jax.nn.gelu(preact).astype(jnp.bfloat16)
    feature_sum = lax.psum(
        jnp.dot(hidden, second_weight, preferred_element_type=jnp.float32), "center"
    )
    squashed = jnp.tanh(feature_sum)
    features = squashed.astype(jnp.bfloat16)
    feat_wide = features.astype(jnp.float32)
    center_wide = centers.astype(jnp.float32)
    feat_norms = jnp.sum(feat_wide * feat_wide, axis=1)
    center_norms = jnp.sum(center_wide * center_wide, axis=1)
    inner_prods = jnp.einsum("tf,cf->tc", features, centers, preferred_element_type=jnp.float32)
    sq_dist = feat_norms[:, None] + center_norms[None, :] - 2.0 * inner_prods
    kernel = jnp.exp(-8.0 * sq_dist / feat_width).astype(jnp.bfloat16)
    pred_part = jnp.dot(kernel, coefficients, preferred_element_type=jnp.float32)
    kernel_grad = jnp.einsum(
        "to,co->tc", cotangent, coefficients, preferred_element_type=jnp.float32
    )
    weighted = kernel_grad * kernel.astype(jnp.float32)
    weighted_low = weighted.astype(jnp.bfloat16)
    feat_grad_part = -factor * (
        jnp.sum(weighted, axis=1)[:, None] * feat_wide
        - jnp.dot(weighted_low, centers, preferred_element_type=jnp.float32)
    )
    center_grad = -factor * (
        jnp.sum(weighted, axis=0)[:, None] * center_wide
        - jnp.einsum("tc,tf->cf", weighted_low, features, preferred_element_type=jnp.float32)
    )
    coef_grad = jnp.einsum("tc,to->co", kernel, cotangent, preferred_element_type=jnp.float32)
    predictions = lax.psum_scatter(
        pred_part.astype(jnp.bfloat16), "center", scatter_dimension=0, tiled=True
    ).astype(jnp.float32)
    feature_grad = lax.psum(feat_grad_part.astype(jnp.bfloat16), "center").astype(jnp.float32)
    phi_grad = (feature_grad * (1.0 - squashed * squashed)).astype(jnp.bfloat16)
    second_grad = jnp.einsum("th,tf->hf", hidden, phi_grad, preferred_element_type=jnp.float32)
    hidden_grad = jnp.einsum(
        "tf,hf->th", phi_grad, second_weight, preferred_element_type=jnp.float32
    )
    unused, pullback = jax.vjp(jax.nn.gelu, preact)
    preact_grad = pullback(hidden_grad)[0]
    bias_grad = jnp.sum(preact_grad, axis=0)
    preact_low = preact_grad.astype(jnp.bfloat16)
    first_grad = jnp.einsum("ti,th->ih", gathered, preact_low, preferred_element_type=jnp.float32)
    first_grad, second_grad, center_grad = (
        lax.psum_scatter(
            first_grad.astype(jnp.bfloat16), "dp", scatter_dimension=0, tiled=True
        ).astype(jnp.float32),
        lax.psum_scatter(
            second_grad.astype(jnp.bfloat16), "dp", scatter_dimension=1, tiled=True
        ).astype(jnp.float32),
        lax.psum_scatter(
            center_grad.astype(jnp.bfloat16), "dp", scatter_dimension=1, tiled=True
        ).astype(jnp.float32),
    )
    bias_grad, coef_grad = (
        lax.psum(bias_grad.astype(jnp.bfloat16), "dp").astype(jnp.float32),
        lax.psum(coef_grad.astype(jnp.bfloat16), "dp").astype(jnp.float32),
    )
    return (predictions, first_grad, bias_grad, second_grad, center_grad, coef_grad)


def solution(mesh):
    placed = (
        P("dp", "center"),
        P(None, "center"),
        P("center"),
        P("center", None),
        P("center", None),
        P("center", None),
        P("dp", None),
    )
    return jax.shard_map(
        body,
        mesh=mesh,
        in_specs=placed,
        out_specs=(
            P(("dp", "center"), None),
            P("dp", "center"),
            P("center"),
            P("center", "dp"),
            P("center", "dp"),
            P("center", None),
        ),
        check_vma=False,
    )
```

profile of v0, /device:TPU:0, one launch (start us, length us, event | category | flops | bytes accessed | tf_op | source)
XLA Modules:
  0.0 502.4 jit_solution(10667676744632239562)
XLA Ops:
  7.2 0.0 copy-start
  7.2 0.0 all-gather.2.cloned.1.call-start
  7.2 0.7 all-gather.2.cloned.1.call-update
  7.9 0.0 all-reduce.3.cloned.1.call-start
  8.0 67.4 %all-gather.2.cloned.1.call-done = bf16[1024,2048]{0,1:T(8,128)(2,1)} async-done(((bf16[1024,64]{0,1:T(8,128)(2,1)}), bf16[1024,2048]{0,1:T(8,128)(2,1)}) %all-gather.2.cloned.1.call-update) | async-done | bytes 4194320 | tf_op jit(solution)/shard_map/all_gather | solution.py:10
  75.3 3.1 convolution_add_fusion
  78.4 1.8 fusion.25
  80.2 0.0 all-reduce.3.cloned.1.call-update
  80.2 0.0 reduce-scatter.2.cloned.1.call-start
  80.3 0.5 fusion
  80.8 133.9 %all-reduce.3.cloned.1.call-done = f32[1024,512]{1,0:T(8,128)} async-done(((f32[1024,512]{1,0:T(8,128)}), f32[1024,512]{1,0:T(8,128)}) %all-reduce.3.cloned.1.call-update) | async-done | bytes 2097168 | tf_op jit(solution)/shard_map/psum | solution.py:13
  214.7 2.0 fusion.8
  216.7 2.9 exponential_convert_fusion
  219.6 2.0 copy-done.3
  221.6 2.0 convolution_convert_fusion.2
  223.6 0.0 reduce-scatter.2.cloned.1.call-update
  223.6 0.2 all-reduce.5.cloned.1.call-start
  223.8 3.9 fusion.26
  227.7 1.9 copy-done.10
  229.7 0.0 copy-done.7
  229.7 3.3 fusion.11
  233.0 0.0 all-reduce.5.cloned.1.call-update
  233.0 7.2 %fusion.4 = f32[2048,512]{1,0:T(8,128)} fusion(bf16[1024,512]{1,0:T(8,128)(2,1)} %copy-done.6, bf16[2048,512]{1,0:T(8,128)(2,1)S(1)} %copy-done.5, f32[2048]{0:T(1024)S(1)} %get-tuple-element.6, bf16[1024,2048]{1,0:T(8,128)(2,1)} %copy-done.10), kind=kOutput, calls=%fused_computation.8 | convolution fusion | flops 2153775104 | bytes 11542528 | tf_op jit(solution)/shard_map/tc,tf->cf/dot_general | solution.py:37
  240.2 1.6 fusion.5
  241.8 116.3 %reduce-scatter.2.cloned.1.call-done = bf16[32,100]{1,0:T(8,128)(2,1)} async-done(((bf16[1024,100]{1,0:T(8,128)(2,1)}), bf16[32,100]{1,0:T(8,128)(2,1)}) %reduce-scatter.2.cloned.1.call-update) | async-done | bytes 6416 | tf_op jit(solution)/shard_map/reduce_scatter | solution.py:40
  358.1 1.3 convert_element_type.79
  359.4 130.3 %all-reduce.5.cloned.1.call-done = bf16[1024,512]{1,0:T(8,128)(2,1)} async-done(((bf16[1024,512]{1,0:T(8,128)(2,1)}), bf16[1024,512]{1,0:T(8,128)(2,1)}) %all-reduce.5.cloned.1.call-update) | async-done | bytes 1048592 | tf_op jit(solution)/shard_map/psum | solution.py:43
  489.7 1.8 multiply_convert_fusion
  491.6 1.0 fusion.17
  492.5 0.6 fusion.27
  493.1 0.5 convert_element_type.160
  493.6 2.2 fusion.7
  (18 shorter events, 0.0 us)
Async XLA Ops:
  7.2 214.4 %copy-start = (bf16[2048,100]{0,1:T(8,128)(2,1)S(1)}, bf16[2048,100]{0,1:T(8,128)(2,1)}, u32[]{:S(2)}) copy-start(bf16[2048,100]{0,1:T(8,128)(2,1)} %param.12) | copy-start | bytes 1228804
  7.2 71.2 %copy-start.9 = (bf16[64,512]{1,0:T(8,128)(2,1)S(1)}, bf16[64,512]{1,0:T(8,128)(2,1)}, u32[]{:S(2)}) copy-start(bf16[64,512]{1,0:T(8,128)(2,1)} %param.10) | copy-start | bytes 196612
  7.2 68.1 %all-gather.2.cloned.1.call-start = ((), (), s32[]{:S(2)}) async-start(), calls=%async_computation.1 | async-start | bytes 4325376 | tf_op jit(solution)/shard_map/all_gather | solution.py:10
  7.9 72.4 %copy-start.5 = (bf16[2048,512]{1,0:T(8,128)(2,1)S(1)}, bf16[2048,512]{1,0:T(8,128)(2,1)}, u32[]{:S(2)}) copy-start(bf16[2048,512]{1,0:T(8,128)(2,1)} %param.11) | copy-start | bytes 6291460
  7.9 206.8 %all-reduce.3.cloned.1.call-start = ((), (), s32[]{:S(2)}) async-start(), calls=%async_computation.2 | async-start | bytes 4194304 | tf_op jit(solution)/shard_map/psum | solution.py:13
  80.2 277.9 %reduce-scatter.2.cloned.1.call-start = ((), (), s32[]{:S(2)}) async-start(), calls=%async_computation.3 | async-start | bytes 270336 | tf_op jit(solution)/shard_map/reduce_scatter | solution.py:40
  216.7 2.9 copy-start.6
  219.6 2.0 copy-start.3
  221.6 2.2 copy-start.8
  223.6 266.1 %all-reduce.5.cloned.1.call-start = ((), (), s32[]{:S(2)}) async-start(), calls=%async_computation.4 | async-start | bytes 2097152 | tf_op jit(solution)/shard_map/psum | solution.py:43
  223.8 5.9 %copy-start.7 = (bf16[1024,512]{1,0:T(8,128)(2,1)S(1)}, bf16[1024,512]{1,0:T(8,128)(2,1)}, u32[]{:S(2)}) copy-start(bf16[1024,512]{1,0:T(8,128)(2,1)} %copy-done.6) | copy-start | bytes 3145732
  227.7 2.0 copy-start.10
  233.0 7.2 %copy-start.4 = (bf16[1024,2048]{1,0:T(8,128)(2,1)S(1)}, bf16[1024,2048]{1,0:T(8,128)(2,1)}, u32[]{:S(2)}) copy-start(bf16[1024,2048]{1,0:T(8,128)(2,1)} %copy-done.3) | copy-start | bytes 12582916
  240.2 249.5 %copy-start.2 = (f32[1024,512]{1,0:T(8,128)S(1)}, f32[1024,512]{1,0:T(8,128)}, u32[]{:S(2)}) copy-start(f32[1024,512]{1,0:T(8,128)} %all-reduce.3.cloned.1.call-done) | copy-start | bytes 6291460
  489.7 3.9 copy-start.1
Sparse Core Ops, SparseCore 0:
  10.9 64.4 all-gather.1
  81.2 133.4 all-reduce.2
  223.7 134.3 reduce-scatter.1
  363.2 126.5 all-reduce.4
where the time goes:
time: 503 us; the launch traced here: 502 us
  waiting for transfers between devices  449 us (89%)
  matrix products  29.4 us (6%)
  between operations  13.9 us (3%)
  other arithmetic  6.12 us (1%)
    psum x1, waiting for transfers between devices, body(): lax.psum(jnp.dot(hidden, second_weight, preferred_element_type=jnp.float3...  134 us
    psum x1, waiting for transfers between devices, body(): lax.psum(feat_grad_part.astype(jnp.bfloat16), 'center').astype(jnp.float32)  130 us
    reduce_scatter x1, waiting for transfers between devices, body(): lax.psum_scatter(pred_part.astype(jnp.bfloat16), 'center', scatter_dimens...  116 us
    all_gather x1, waiting for transfers between devices, body(): gathered = lax.all_gather(embeddings, 'center', axis=1, tiled=True)  67.4 us
  transfers between devices with their start and end apart: 4, of which 4 were waited for; matrix products, arithmetic and copies ran while one was open for 4% of the time, Pallas kernels for 0%

commit v1 on v0

--- a/solution.py
+++ b/solution.py
@@ -40,7 +40,9 @@
     predictions = lax.psum_scatter(
         pred_part.astype(jnp.bfloat16), "center", scatter_dimension=0, tiled=True
     ).astype(jnp.float32)
-    feature_grad = lax.psum(feat_grad_part.astype(jnp.bfloat16), "center").astype(jnp.float32)
+    feature_grad = jnp.sum(
+        lax.all_gather(feat_grad_part.astype(jnp.bfloat16), "center"), axis=0
+    ).astype(jnp.float32)
     phi_grad = (feature_grad * (1.0 - squashed * squashed)).astype(jnp.bfloat16)
     second_grad = jnp.einsum("th,tf->hf", hidden, phi_grad, preferred_element_type=jnp.float32)
     hidden_grad = jnp.einsum(

time: 503 us -> 576 us (1.15)
  waiting for transfers between devices: 449 us -> 510 us
  other arithmetic: 6.12 us -> 18.6 us
    all_gather x0 -> x1, waiting for transfers between devices: none -> 191 us  [body(): lax.all_gather(feat_grad_part.astype(jnp.bfloat16), 'center')]
    psum x1 -> x0, waiting for transfers between devices: 130 us -> none  [body(): lax.psum(feat_grad_part.astype(jnp.bfloat16), 'center').astype(jnp.float32)]
    reduce_sum x0 -> x1, other arithmetic: none -> 12.5 us  [body(): jnp.sum(lax.all_gather(feat_grad_part.astype(jnp.bfloat16), 'center'), ax...]
  transfers between devices with their start and end apart: 4 -> 4, of which waited for: 4 -> 4; matrix products, arithmetic and copies ran while one was open for 4% -> 3% of each run, Pallas kernels for 0% -> 0%
where the time goes in v1:
time: 576 us
  waiting for transfers between devices  510 us (89%)
  matrix products  29.1 us (5%)
  other arithmetic  18.6 us (3%)
  between operations  13.9 us (2%)
    all_gather x1, waiting for transfers between devices, body(): lax.all_gather(feat_grad_part.astype(jnp.bfloat16), 'center')  191 us
    psum x1, waiting for transfers between devices, body(): lax.psum(jnp.dot(hidden, second_weight, preferred_element_type=jnp.float3...  134 us
    reduce_scatter x1, waiting for transfers between devices, body(): lax.psum_scatter(pred_part.astype(jnp.bfloat16), 'center', scatter_dimens...  117 us
    all_gather x1, waiting for transfers between devices, body(): gathered = lax.all_gather(embeddings, 'center', axis=1, tiled=True)  67.4 us
    reduce_sum x1, other arithmetic, body(): jnp.sum(lax.all_gather(feat_grad_part.astype(jnp.bfloat16), 'center'), ax...  12.5 us
  transfers between devices with their start and end apart: 4, of which 4 were waited for; matrix products, arithmetic and copies ran while one was open for 3% of the time, Pallas kernels for 0%

profile of v1, /device:TPU:0, one launch (start us, length us, event | category | flops | bytes accessed | tf_op | source)
XLA Modules:
  0.0 576.1 jit_solution(14120177396860181747)
XLA Ops:
  7.2 0.0 copy-start
  7.2 0.0 all-gather.4.cloned.1.call-start
  7.2 0.7 all-gather.4.cloned.1.call-update
  7.9 0.0 all-reduce.2.cloned.1.call-start
  8.0 67.4 %all-gather.4.cloned.1.call-done = bf16[1024,2048]{0,1:T(8,128)(2,1)} async-done(((bf16[1024,64]{0,1:T(8,128)(2,1)}), bf16[1024,2048]{0,1:T(8,128)(2,1)}) %all-gather.4.cloned.1.call-update) | async-done | bytes 4194320 | tf_op jit(solution)/shard_map/all_gather | solution.py:10
  75.3 3.1 convolution_add_fusion
  78.4 1.8 fusion.25
  80.2 0.0 all-reduce.2.cloned.1.call-update
  80.2 0.0 reduce-scatter.2.cloned.1.call-start
  80.3 0.5 fusion
  80.8 133.9 %all-reduce.2.cloned.1.call-done = f32[1024,512]{1,0:T(8,128)} async-done(((f32[1024,512]{1,0:T(8,128)}), f32[1024,512]{1,0:T(8,128)}) %all-reduce.2.cloned.1.call-update) | async-done | bytes 2097168 | tf_op jit(solution)/shard_map/psum | solution.py:13
  214.7 2.0 fusion.8
  216.7 2.9 exponential_convert_fusion
  219.6 2.0 copy-done.3
  221.7 2.0 convolution_convert_fusion.2
  223.6 0.0 reduce-scatter.2.cloned.1.call-update
  223.6 0.2 all-gather.6.cloned.1.call-start
  223.9 3.9 fusion.26
  227.8 2.0 copy-done.10
  229.7 3.3 fusion.11
  233.0 0.0 all-gather.6.cloned.1.call-update
  233.1 3.9 fusion.5
  237.0 4.6 fusion.4
  241.6 116.6 %reduce-scatter.2.cloned.1.call-done = bf16[32,100]{1,0:T(8,128)(2,1)} async-done(((bf16[1024,100]{1,0:T(8,128)(2,1)}), bf16[32,100]{1,0:T(8,128)(2,1)}) %reduce-scatter.2.cloned.1.call-update) | async-done | bytes 6416 | tf_op jit(solution)/shard_map/reduce_scatter | solution.py:40
  358.2 1.3 convert_element_type.81
  359.5 191.5 %all-gather.6.cloned.1.call-done = bf16[32768,512]{1,0:T(8,128)(2,1)} async-done(((bf16[1024,512]{1,0:T(8,128)(2,1)}), bf16[32768,512]{1,0:T(8,128)(2,1)}) %all-gather.6.cloned.1.call-update) | async-done | bytes 33554448 | tf_op jit(solution)/shard_map/all_gather | solution.py:44
  550.9 12.5 %reduce_sum.60 = bf16[1024,512]{1,0:T(8,128)(2,1)} reduce(bf16[32,1024,512]{2,1,0:T(8,128)(2,1)} %bitcast.23, bf16[]{:T(256)} %constant.24.clone.1), dimensions={0}, to_apply=%region_5.0 | reduce | flops 16252928 | bytes 34603008 | tf_op jit(solution)/shard_map/reduce_sum | solution.py:43
  563.4 1.8 multiply_convert_fusion
  565.3 1.0 fusion.17
  566.2 0.6 fusion.27
  566.8 0.5 convert_element_type.162
  567.3 2.2 fusion.7
  (21 shorter events, 0.0 us)
Async XLA Ops:
  7.2 214.5 %copy-start = (bf16[2048,100]{0,1:T(8,128)(2,1)S(1)}, bf16[2048,100]{0,1:T(8,128)(2,1)}, u32[]{:S(2)}) copy-start(bf16[2048,100]{0,1:T(8,128)(2,1)} %param.12) | copy-start | bytes 1228804
  7.2 71.2 %copy-start.9 = (bf16[64,512]{1,0:T(8,128)(2,1)S(1)}, bf16[64,512]{1,0:T(8,128)(2,1)}, u32[]{:S(2)}) copy-start(bf16[64,512]{1,0:T(8,128)(2,1)} %param.10) | copy-start | bytes 196612
  7.2 68.1 %all-gather.4.cloned.1.call-start = ((), (), s32[]{:S(2)}) async-start(), calls=%async_computation.1 | async-start | bytes 4325376 | tf_op jit(solution)/shard_map/all_gather | solution.py:10
  7.9 72.4 %copy-start.4 = (bf16[2048,512]{1,0:T(8,128)(2,1)S(1)}, bf16[2048,512]{1,0:T(8,128)(2,1)}, u32[]{:S(2)}) copy-start(bf16[2048,512]{1,0:T(8,128)(2,1)} %param.11) | copy-start | bytes 6291460
  7.9 206.8 %all-reduce.2.cloned.1.call-start = ((), (), s32[]{:S(2)}) async-start(), calls=%async_computation.2 | async-start | bytes 4194304 | tf_op jit(solution)/shard_map/psum | solution.py:13
  80.2 277.9 %reduce-scatter.2.cloned.1.call-start = ((), (), s32[]{:S(2)}) async-start(), calls=%async_computation.3 | async-start | bytes 270336 | tf_op jit(solution)/shard_map/reduce_scatter | solution.py:40
  216.7 2.9 copy-start.5
  219.6 2.0 copy-start.3
  221.7 2.2 copy-start.8
  223.6 327.3 %all-gather.6.cloned.1.call-start = ((), (), s32[]{:S(2)}) async-start(), calls=%async_computation.4 | async-start | bytes 34603008 | tf_op jit(solution)/shard_map/all_gather | solution.py:44
  223.9 5.9 %copy-start.6 = (bf16[1024,512]{1,0:T(8,128)(2,1)S(1)}, bf16[1024,512]{1,0:T(8,128)(2,1)}, u32[]{:S(2)}) copy-start(bf16[1024,512]{1,0:T(8,128)(2,1)} %copy-done.5) | copy-start | bytes 3145732
  227.8 2.0 copy-start.10
  233.1 4.0 copy-start.7
  233.1 4.0 copy-start.11
  550.9 12.5 %copy-start.2 = (f32[1024,512]{1,0:T(8,128)S(1)}, f32[1024,512]{1,0:T(8,128)}, u32[]{:S(2)}) copy-start(f32[1024,512]{1,0:T(8,128)} %all-reduce.2.cloned.1.call-done) | copy-start | bytes 6291460
  563.4 3.9 copy-start.1
Sparse Core Ops, SparseCore 0:
  10.9 64.4 all-gather.3
  81.2 133.4 all-reduce.1
  223.8 134.3 reduce-scatter.1
  360.9 190.0 all-gather.5

commit v2 on v0

--- a/solution.py
+++ b/solution.py
@@ -7,7 +7,7 @@
 def body(embeddings, first_weight, first_bias, second_weight, centers, coefficients, cotangent):
     feat_width = centers.shape[1]
     factor = 16.0 / feat_width
-    gathered = lax.all_gather(embeddings, "center", axis=1, tiled=True)
+    gathered = jnp.concatenate(lax.all_gather(embeddings, "center"), axis=1)
     preact = jnp.dot(gathered, first_weight, preferred_element_type=jnp.float32) + first_bias
     hidden = jax.nn.gelu(preact).astype(jnp.bfloat16)
     feature_sum = lax.psum(

time: 503 us -> 508 us (level)
  local copies, waits for them, and re-layouts: 3.96 us -> 12.9 us
    unnamed x22 -> x29, local copies, waits for them, and re-layouts: 3.96 us -> 10.5 us
where the time goes in v2:
time: 508 us
  waiting for transfers between devices  447 us (88%)
  matrix products  27.2 us (5%)
  between operations  13.9 us (3%)
  local copies, waits for them, and re-layouts  12.9 us (3%)
  other arithmetic  6.11 us (1%)
    psum x1, waiting for transfers between devices, body(): lax.psum(jnp.dot(hidden, second_weight, preferred_element_type=jnp.float3...  133 us
    psum x1, waiting for transfers between devices, body(): lax.psum(feat_grad_part.astype(jnp.bfloat16), 'center').astype(jnp.float32)  130 us
    reduce_scatter x1, waiting for transfers between devices, body(): lax.psum_scatter(pred_part.astype(jnp.bfloat16), 'center', scatter_dimens...  116 us
    all_gather x1, waiting for transfers between devices, body(): gathered = jnp.concatenate(lax.all_gather(embeddings, 'center'), axis=1)  67.4 us
    unnamed x29, local copies, waits for them, and re-layouts  10.5 us
  transfers between devices with their start and end apart: 4, of which 4 were waited for; matrix products, arithmetic and copies ran while one was open for 4% of the time, Pallas kernels for 0%

profile of v2, /device:TPU:0, one launch (start us, length us, event | category | flops | bytes accessed | tf_op | source)
XLA Modules:
  0.0 507.8 jit_solution(16674384829793613967)
XLA Ops:
  7.2 0.0 all-gather.3.cloned.1.call-start
  7.2 0.7 all-gather.3.cloned.1.call-update
  7.9 0.0 all-reduce.3.cloned.1.call-start
  8.0 67.4 %all-gather.3.cloned.1.call-done = bf16[32768,64]{0,1:T(8,128)(2,1)} async-done(((bf16[1024,64]{0,1:T(8,128)(2,1)}), bf16[32768,64]{0,1:T(8,128)(2,1)}) %all-gather.3.cloned.1.call-update) | async-done | bytes 4194320 | tf_op jit(solution)/shard_map/all_gather | solution.py:10
  75.4 4.6 copy.14
  80.0 2.3 copy.13
  82.4 1.9 copy-done.1
  84.3 0.8 convolution_add_fusion
  85.2 1.8 fusion.25
  87.0 0.0 all-reduce.3.cloned.1.call-update
  87.0 0.0 reduce-scatter.2.cloned.1.call-start
  87.1 0.5 fusion
  87.5 133.0 %all-reduce.3.cloned.1.call-done = f32[1024,512]{1,0:T(8,128)} async-done(((f32[1024,512]{1,0:T(8,128)}), f32[1024,512]{1,0:T(8,128)}) %all-reduce.3.cloned.1.call-update) | async-done | bytes 2097168 | tf_op jit(solution)/shard_map/psum | solution.py:13
  220.5 2.0 fusion.8
  222.5 2.9 exponential_convert_fusion
  225.5 2.0 copy-done.4
  227.4 2.0 convolution_convert_fusion.2
  229.4 0.2 all-reduce.5.cloned.1.call-start
  229.7 3.9 fusion.26
  233.5 2.0 copy-done.13
  235.5 3.3 fusion.11
  238.8 0.0 all-reduce.5.cloned.1.call-update
  238.9 7.2 %fusion.4 = f32[2048,512]{1,0:T(8,128)} fusion(bf16[1024,512]{1,0:T(8,128)(2,1)} %copy-done.7, bf16[2048,512]{1,0:T(8,128)(2,1)S(1)} %copy-done.6, f32[2048]{0:T(1024)S(1)} %get-tuple-element.6, bf16[1024,2048]{1,0:T(8,128)(2,1)} %copy-done.13), kind=kOutput, calls=%fused_computation.8 | convolution fusion | flops 2153775104 | bytes 11542528 | tf_op jit(solution)/shard_map/tc,tf->cf/dot_general | solution.py:37
  246.0 1.6 fusion.5
  247.7 115.8 %reduce-scatter.2.cloned.1.call-done = bf16[32,100]{1,0:T(8,128)(2,1)} async-done(((bf16[1024,100]{1,0:T(8,128)(2,1)}), bf16[32,100]{1,0:T(8,128)(2,1)}) %reduce-scatter.2.cloned.1.call-update) | async-done | bytes 6416 | tf_op jit(solution)/shard_map/reduce_scatter | solution.py:40
  363.5 1.3 convert_element_type.79
  364.8 130.3 %all-reduce.5.cloned.1.call-done = bf16[1024,512]{1,0:T(8,128)(2,1)} async-done(((bf16[1024,512]{1,0:T(8,128)(2,1)}), bf16[1024,512]{1,0:T(8,128)(2,1)}) %all-reduce.5.cloned.1.call-update) | async-done | bytes 1048592 | tf_op jit(solution)/shard_map/psum | solution.py:43
  495.2 1.8 multiply_convert_fusion
  497.0 1.0 fusion.17
  498.0 0.6 fusion.27
  498.6 2.2 fusion.7
  500.7 0.5 convert_element_type.160
  (26 shorter events, 0.1 us)
Async XLA Ops:
  7.2 220.3 %copy-start = (bf16[2048,100]{0,1:T(8,128)(2,1)S(1)}, bf16[2048,100]{0,1:T(8,128)(2,1)}, u32[]{:S(2)}) copy-start(bf16[2048,100]{0,1:T(8,128)(2,1)} %param.12) | copy-start | bytes 1228804
  7.2 68.2 %all-gather.3.cloned.1.call-start = ((), (), s32[]{:S(2)}) async-start(), calls=%async_computation.4 | async-start | bytes 4325376 | tf_op jit(solution)/shard_map/all_gather | solution.py:10
  7.9 212.6 %all-reduce.3.cloned.1.call-start = ((), (), s32[]{:S(2)}) async-start(), calls=%async_computation.1 | async-start | bytes 4194304 | tf_op jit(solution)/shard_map/psum | solution.py:13
  80.0 4.3 copy-start.9
  80.0 4.3 copy-start.12
  82.4 1.9 copy-start.1
  82.4 2.8 copy-start.11
  84.3 2.7 copy-start.6
  87.0 276.5 %reduce-scatter.2.cloned.1.call-start = ((), (), s32[]{:S(2)}) async-start(), calls=%async_computation.2 | async-start | bytes 270336 | tf_op jit(solution)/shard_map/reduce_scatter | solution.py:40
  222.5 2.9 copy-start.7
  225.5 2.0 copy-start.4
  227.4 2.2 copy-start.10
  229.4 265.8 %all-reduce.5.cloned.1.call-start = ((), (), s32[]{:S(2)}) async-start(), calls=%async_computation.3 | async-start | bytes 2097152 | tf_op jit(solution)/shard_map/psum | solution.py:43
  229.7 5.8 %copy-start.8 = (bf16[1024,512]{1,0:T(8,128)(2,1)S(1)}, bf16[1024,512]{1,0:T(8,128)(2,1)}, u32[]{:S(2)}) copy-start(bf16[1024,512]{1,0:T(8,128)(2,1)} %copy-done.7) | copy-start | bytes 3145732
  233.5 2.0 copy-start.13
  238.8 7.2 %copy-start.5 = (bf16[1024,2048]{1,0:T(8,128)(2,1)S(1)}, bf16[1024,2048]{1,0:T(8,128)(2,1)}, u32[]{:S(2)}) copy-start(bf16[1024,2048]{1,0:T(8,128)(2,1)} %copy-done.4) | copy-start | bytes 12582916
  246.0 249.1 %copy-start.3 = (f32[1024,512]{1,0:T(8,128)S(1)}, f32[1024,512]{1,0:T(8,128)}, u32[]{:S(2)}) copy-start(f32[1024,512]{1,0:T(8,128)} %all-reduce.3.cloned.1.call-done) | copy-start | bytes 6291460
  495.2 3.4 copy-start.2
Sparse Core Ops, SparseCore 0:
  10.9 64.4 all-gather.2
  87.1 133.3 all-reduce.2
  229.5 133.9 reduce-scatter.1
  368.6 126.5 all-reduce.4
